TPU v7x, 256 devices: a whole 4x4x8 slice. The times are simulated.
256 devices in a mesh: cells: 64 (over z, y, core), tm: 4 (over x).
Axes of the slice: x: 4, y: 4, z: 8, core: 2. Of those that a mesh axis runs over, the one named last changes fastest.
Arguments:
- attitude: float32 [4, 65536], P(None, ('cells', 'tm')), may hold values from -6 to 6
- star_partials: float32 [5, 64, 131072], P(None, None, ('cells', 'tm')), may hold values from -6 to 6
- attitude_partials: float32 [4, 64, 131072], P(None, None, ('cells', 'tm')), may hold values from -6 to 6
- observed: float32 [64, 131072], P(None, ('cells', 'tm')), may hold values from -6 to 6
- phase: float32 [64, 131072], P(None, ('cells', 'tm')), may hold values from 0 to 1
- knot_offset: int32 [64, 131072], P(None, ('cells', 'tm')), may hold values from 0 to 12
- cell_counts: int32 [1024], P(('cells', 'tm')), may hold values from 40 to 64, as said below
- interval_owner: int32 [1024, 64, 1], P(('cells', 'tm')), may hold values from 0 to 255; in each aligned block of 256 rows (0 to 255, 256 to 511, ..., all dimensions but the last counted through in order) at most 2 rows name the same one
- block_slot: int32 [1024, 64], P(('cells', 'tm')), may hold values from 0 to 15
Outputs:
- star_step: float32 [5, 131072], P(None, ('cells', 'tm'))
- attitude_step: float32 [4, 65536], P(None, ('cells', 'tm'))
Inputs may be any that keep to these rules, and one draw needn't show every extreme that they name: `interval_owner`: among the 256 transits of the cells of one device no owner is named more than 2 times, and in every draw some owner is named exactly 2 times by the transits of some device. Transits that are not live are listed too. `cell_counts`: some cell has all 64 transits live in every draw.
All inputs are finite; a program needn't handle non-finite values.
Results may differ from a plain program's by a relative error of at most 0.0003.
Values sent between devices are 32-bit elements; how exact they have to be, the bound alone decides.
A program may use at most 128 MiB of HBM per device.

v0:
```python
import jax
import jax.numpy as jnp
from jax import lax
from jax.sharding import PartitionSpec as P

CS = 128
KB = 16
ITERS = 6
smoothing = 16.0
damping = 2.0
relaxation = 0.5
star_prior = 1.0
highest = lax.Precision.HIGHEST


def padded_2(shard, sides, width):
    for axis, dim in sides:
        size, length = (lax.axis_size(axis), shard.shape[dim])
        up = [(i, (i + 1) % size) for i in range(size - 1)]
        down = [(j, i) for i, j in up]
        last = lax.slice_in_dim(shard, length - width, length, axis=dim)
        leading = lax.slice_in_dim(shard, 0, width, axis=dim)
        before = lax.ppermute(last, axis, up)
        after = lax.ppermute(leading, axis, down)
        shard = jnp.concatenate([before, shard, after], axis=dim)
    return shard


def spline_basis(phase):
    square = phase * phase
    cube = square * phase
    rest = 1.0 - phase
    return (
        rest * rest * rest / 6.0,
        (3.0 * cube - 6.0 * square + 4.0) / 6.0,
        (-3.0 * cube + 3.0 * square + 3.0 * phase + 1.0) / 6.0,
        cube / 6.0,
    )


def design_rows(phase, knot_offset, partials, live):
    knots = lax.broadcasted_iota(jnp.int32, (KB, 1), 0)
    basis = spline_basis(phase)
    spread = jnp.zeros(phase.shape[:-1] + (KB, phase.shape[-1]), jnp.float32)
    for order in range(4):
        hit = knots == knot_offset[..., None, :] + order
        spread = spread + jnp.where(hit, basis[order][..., None, :], 0.0)
    spread = spread * live[..., None, None]
    return jnp.moveaxis(partials, 0, -2)[..., :, None, :] * spread[..., None, :, :]


def cholesky_factor(matrix, size):
    lower = [[None for column in range(size)] for row in range(size)]
    for column in range(size):
        total = matrix[column][column]
        for inner in range(column):
            total = total - lower[column][inner] * lower[column][inner]
        pivot = jnp.sqrt(total)
        lower[column][column] = pivot
        for row in range(column + 1, size):
            accum = matrix[row][column]
            for inner in range(column):
                accum = accum - lower[row][inner] * lower[column][inner]
            lower[row][column] = accum / pivot
    return lower


def cholesky_solve(lower, rhs, size):
    forward = []
    for row in range(size):
        accum = rhs[row]
        for inner in range(row):
            accum = accum - lower[row][inner] * forward[inner]
        forward.append(accum / lower[row][row])
    answer = [None for row in range(size)]
    for row in reversed(range(size)):
        accum = forward[row]
        for inner in range(row + 1, size):
            accum = accum - lower[inner][row] * answer[inner]
        answer[row] = accum / lower[row][row]
    return answer


def star_update(partials, first, live):
    normal = [
        [
            jnp.sum(live * partials[row] * partials[column], axis=0)
            + (star_prior if row == column else 0.0)
            for column in range(5)
        ]
        for row in range(5)
    ]
    rhs = [jnp.sum(partials[row] * first, axis=0) for row in range(5)]
    lower = cholesky_factor(normal, 5)
    step = cholesky_solve(lower, rhs, 5)
    fitted = partials[0] * step[0]
    for row in range(1, 5):
        fitted = fitted + partials[row] * step[row]
    return (jnp.stack(step), first - live * fitted)


def dense_to_band(dense):
    pieces = []
    for shift in range(4):
        diagonal = jnp.diagonal(dense, offset=shift, axis1=2, axis2=4)
        filler = jnp.zeros(diagonal.shape[:-1] + (shift,), jnp.float32)
        pieces.append(jnp.concatenate([diagonal, filler], axis=-1))
    return jnp.stack(pieces, axis=-2)


def band_apply(band, vector):
    result = jnp.einsum("bmna,nba->mba", band[:, :, :, 0, :], vector, precision=highest)
    for shift in range(1, 4):
        filler = jnp.zeros(vector.shape[:-1] + (shift,), jnp.float32)
        ahead = jnp.concatenate([vector[..., shift:], filler], axis=-1)
        result = result + jnp.einsum(
            "bmna,nba->mba", band[:, :, :, shift, :], ahead, precision=highest
        )
        lagged = jnp.einsum("bnma,nba->mba", band[:, :, :, shift, :], vector, precision=highest)
        result = result + jnp.concatenate([filler, lagged[..., : KB - shift]], axis=-1)
    return result


def diagonal_factor(band):
    shifted = 2.0 * smoothing + damping
    entries = [
        [band[:, row, column, 0, :] + (shifted if row == column else 0.0) for column in range(4)]
        for row in range(4)
    ]
    return cholesky_factor(entries, 4)


def sweep(band, lower, gradient, solution, padded):
    count = band.shape[0]
    applied = band_apply(band, solution.reshape(4, count, KB))
    regular = smoothing * (2.0 * solution - padded[:, :-2] - padded[:, 2:]) + damping * solution
    misfit = gradient - applied - regular.reshape(4, count, KB)
    correction = cholesky_solve(lower, [misfit[row] for row in range(4)], 4)
    return solution + relaxation * jnp.stack(correction).reshape(4, count * KB)


def cell_work(items):
    cell_phase, cell_offset, cell_axis, cell_star, cell_observed, cell_live, cell_values = items
    rows = design_rows(cell_phase, cell_offset, cell_axis, cell_live)
    predicted = jnp.einsum("tmas,tma->ts", rows, cell_values, precision=highest)
    first = cell_live[:, None] * cell_observed - predicted
    step, second = star_update(cell_star, first, cell_live[:, None])
    gradient = jnp.einsum("tmas,ts->tma", rows, second, precision=highest)
    flat = rows.reshape(rows.shape[0], 4 * KB, rows.shape[-1])
    normal = jnp.einsum("tis,tks->tik", flat, flat, precision=highest).reshape(
        rows.shape[0], 16 * KB * KB
    )
    return (step, normal, gradient.reshape(rows.shape[0], 4 * KB))


def per_device(
    attitude,
    star_partials,
    attitude_partials,
    observed,
    phase,
    knot_offset,
    cell_counts,
    interval_owner,
    block_slot,
):
    cell_groups = lax.axis_size("cells")
    time_groups = lax.axis_size("tm")
    devices = cell_groups * time_groups
    cells_here = cell_counts.shape[0]
    transits = observed.shape[0]
    blocks_here = attitude.shape[1] // KB
    total = cells_here * transits
    capacity = max(2, 3 * total // (2 * devices))
    owners = interval_owner.reshape(total)
    slots = block_slot.reshape(total)
    order = lax.broadcasted_iota(jnp.int32, (total, total), 0)
    other = lax.broadcasted_iota(jnp.int32, (total, total), 1)
    same = (owners[:, None] == owners[None, :]) & (other < order)
    rank = jnp.sum(same.astype(jnp.int32), axis=1)
    position = owners * capacity + rank
    requests = jnp.zeros((devices * capacity,), jnp.int32).at[position].set(slots)
    requested = lax.all_to_all(
        lax.all_to_all(
            requests.reshape(cell_groups, time_groups, capacity),
            "cells",
            split_axis=0,
            concat_axis=0,
            tiled=True,
        ),
        "tm",
        split_axis=1,
        concat_axis=1,
        tiled=True,
    )
    whole = lax.all_gather(attitude, ("cells", "tm"), axis=1, tiled=True)
    global_ids = owners * blocks_here + slots
    values = whole.reshape(4, -1, KB)[:, global_ids, :].transpose(1, 0, 2)
    transit = lax.broadcasted_iota(jnp.int32, (cells_here, transits), 1)
    live = jnp.where(transit < cell_counts[:, None], 1.0, 0.0).astype(jnp.float32)
    items = (
        phase.reshape(transits, cells_here, CS).transpose(1, 0, 2),
        knot_offset.reshape(transits, cells_here, CS).transpose(1, 0, 2),
        attitude_partials.reshape(4, transits, cells_here, CS).transpose(2, 0, 1, 3),
        star_partials.reshape(5, transits, cells_here, CS).transpose(2, 0, 1, 3),
        observed.reshape(transits, cells_here, CS).transpose(1, 0, 2),
        live,
        values.reshape(cells_here, transits, 4, KB),
    )
    steps, normals, gradients = lax.map(cell_work, items)
    payload = normals.reshape(total, normals.shape[-1])
    gradient_rows = gradients.reshape(total, 4 * KB)
    outgoing = (
        jnp.zeros((devices * capacity, payload.shape[1]), jnp.float32).at[position].set(payload)
    )
    outgoing_grad = (
        jnp.zeros((devices * capacity, 4 * KB), jnp.float32).at[position].set(gradient_rows)
    )
    arrived, arrived_grad = (
        lax.all_to_all(
            lax.all_to_all(
                outgoing.reshape(cell_groups, time_groups, capacity, payload.shape[1]),
                "cells",
                split_axis=0,
                concat_axis=0,
                tiled=True,
            ),
            "tm",
            split_axis=1,
            concat_axis=1,
            tiled=True,
        ),
        lax.all_to_all(
            lax.all_to_all(
                outgoing_grad.reshape(cell_groups, time_groups, capacity, 4 * KB),
                "cells",
                split_axis=0,
                concat_axis=0,
                tiled=True,
            ),
            "tm",
            split_axis=1,
            concat_axis=1,
            tiled=True,
        ),
    )
    member_rows = lax.broadcasted_iota(jnp.int32, (blocks_here, devices * capacity), 0)
    member = (member_rows == requested.reshape(1, devices * capacity)).astype(jnp.float32)
    block_normal = jnp.dot(
        member,
        arrived.reshape(devices * capacity, payload.shape[1]),
        precision=highest,
        preferred_element_type=jnp.float32,
    )
    block_grad = jnp.dot(
        member,
        arrived_grad.reshape(devices * capacity, 4 * KB),
        precision=highest,
        preferred_element_type=jnp.float32,
    )
    band = dense_to_band(block_normal.reshape(blocks_here, 4, KB, 4, KB))
    gradient = block_grad.reshape(blocks_here, 4, KB).transpose(1, 0, 2)
    lower = diagonal_factor(band)
    solution = jnp.zeros((4, blocks_here * KB), jnp.float32)
    for index in range(ITERS):
        padded = padded_2(solution, ((("cells", "tm"), 1),), 1)
        solution = sweep(band, lower, gradient, solution, padded)
    star_step = steps.transpose(1, 0, 2).reshape(5, cells_here * CS)
    return (star_step, solution)


def solution(mesh):
    placed = (
        P(None, ("cells", "tm")),
        P(None, None, ("cells", "tm")),
        P(None, None, ("cells", "tm")),
        P(None, ("cells", "tm")),
        P(None, ("cells", "tm")),
        P(None, ("cells", "tm")),
        P(("cells", "tm")),
        P(("cells", "tm"), None, None),
        P(("cells", "tm"), None),
    )
    return jax.shard_map(
        per_device,
        mesh=mesh,
        in_specs=placed,
        out_specs=(P(None, ("cells", "tm")), P(None, ("cells", "tm"))),
        check_vma=False,
    )
```

profile of v0, /device:TPU:127, one launch (start us, length us, event | category | flops | bytes accessed | tf_op | source)
XLA Modules:
  0.0 741.4 jit_solution(1246843753524124529)
XLA Ops:
  8.4 1.4 fusion.207
  11.5 1.4 scatter_custom_fusion
  14.2 10.9 %all-to-all-start = ((s32[64,4,2]{1,2,0:T(2,128)}), s32[64,4,2]{1,2,0:T(2,128)S(1)}, u32[]{:S(2)}, u32[]{:S(2)}) async-start(s32[64,4,2]{1,2,0:T(2,128)} %copy.75), calls=%async_computation | async-start | bytes 131072 | tf_op jit(solution)/shard_map/all_to_all | solution.py:184
  25.9 1.3 fusion.191
  27.2 2.1 reshape.1755
  29.4 2.0 reshape.1757
  33.3 1.6 reshape.1759
  35.7 4.2 all-to-all-start.1
  39.9 75.8 %all-gather.2.cloned.1.call-done = f32[4,65536]{1,0:T(4,128)} async-done(((f32[4,256]{1,0:T(4,128)}), f32[4,65536]{1,0:T(4,128)}) %all-gather.2.cloned.1.call-update) | async-done | bytes 1048592 | tf_op jit(solution)/shard_map/all_gather | solution.py:196
  115.7 7.3 reshape.1760
  123.1 11.8 %copy.67 = f32[4,4096,16]{2,0,1:T(4,128)} copy(f32[4,4096,16]{2,1,0:T(8,128)} %reshape.1760) | data formatting | bytes 2097152 | tf_op jit(solution)/shard_map/reshape | solution.py:198
  134.9 4.4 gather_fusion
  139.5 125.9 %while.14 = (s32[]{:T(128)}, f32[4,5,128]{2,1,0:T(8,128)}, f32[4,64,4096]{2,1,0:T(8,128)}, f32[4,64,64]{2,1,0:T(8,128)}, f32[4,5,64,128]{3,0,2,1:T(4,128)}, /*in...) while((s32[]{:T(128)}, f32[4,5,128]{2,1,0:T(8,128)}, ...), condition=%wide.region_21.22_spmd, body=%wide.region_0.21_spmd.sunk | while | flops 419069696 | bytes 14432589 | solution.py:210
  143.4 2.0 fusion.265
  145.4 1.2 constant_dynamic-slice_fusion.10
  147.6 14.7 %fusion.269 = f32[64,1,4,16]{3,1,2,0:T(1,128)S(1)} fusion(f32[64,128,1,1]{1,2,3,0:T(1,128)S(1)} %bitcast.973, f32[64,16,128]{2,1,0:T(8,128)S(1)} %add_multiply_fusion.2, f32[64,4,128]{2,1,0:T(4,128)S(1)} %bitcast.953), kind=kOutput, calls=%fused_computation.8.clone.1 | convolution fusion | flops 6815744 | bytes 704512 | tf_op jit(solution)/shard_map/while/body/eval_jaxpr/tmas,ts->tma/dot_general | solution.py:148
  163.3 3.4 fusion.268
  174.7 2.0 fusion.265
  176.7 1.2 constant_dynamic-slice_fusion.10
  178.8 14.7 %fusion.269 = f32[64,1,4,16]{3,1,2,0:T(1,128)S(1)} fusion(f32[64,128,1,1]{1,2,3,0:T(1,128)S(1)} %bitcast.973, f32[64,16,128]{2,1,0:T(8,128)S(1)} %add_multiply_fusion.2, f32[64,4,128]{2,1,0:T(4,128)S(1)} %bitcast.953), kind=kOutput, calls=%fused_computation.8.clone.1 | convolution fusion | flops 6815744 | bytes 704512 | tf_op jit(solution)/shard_map/while/body/eval_jaxpr/tmas,ts->tma/dot_general | solution.py:148
  194.6 3.4 fusion.268
  206.0 2.0 fusion.265
  210.2 14.7 %fusion.269 = f32[64,1,4,16]{3,1,2,0:T(1,128)S(1)} fusion(f32[64,128,1,1]{1,2,3,0:T(1,128)S(1)} %bitcast.973, f32[64,16,128]{2,1,0:T(8,128)S(1)} %add_multiply_fusion.2, f32[64,4,128]{2,1,0:T(4,128)S(1)} %bitcast.953), kind=kOutput, calls=%fused_computation.8.clone.1 | convolution fusion | flops 6815744 | bytes 704512 | tf_op jit(solution)/shard_map/while/body/eval_jaxpr/tmas,ts->tma/dot_general | solution.py:148
  225.9 3.4 fusion.268
  237.3 2.0 fusion.265
  241.5 14.7 %fusion.269 = f32[64,1,4,16]{3,1,2,0:T(1,128)S(1)} fusion(f32[64,128,1,1]{1,2,3,0:T(1,128)S(1)} %bitcast.973, f32[64,16,128]{2,1,0:T(8,128)S(1)} %add_multiply_fusion.2, f32[64,4,128]{2,1,0:T(4,128)S(1)} %bitcast.953), kind=kOutput, calls=%fused_computation.8.clone.1 | convolution fusion | flops 6815744 | bytes 704512 | tf_op jit(solution)/shard_map/while/body/eval_jaxpr/tmas,ts->tma/dot_general | solution.py:148
  257.2 3.4 fusion.268
  265.3 1.6 scatter_custom_fusion.1
  267.8 8.8 %all-to-all-start.2 = ((f32[64,1,512]{2,1,0:T(1,128)}), f32[64,1,512]{2,1,0:T(1,128)S(1)}, u32[]{:S(2)}, u32[]{:S(2)}) async-start(f32[64,1,512]{2,1,0:T(1,128)} %reshape.1951), calls=%async_computation.2 | async-start | bytes 262144 | tf_op jit(solution)/shard_map/all_to_all | solution.py:234
  276.7 8.2 %scatter_custom_fusion.2 = f32[512,4096]{1,0:T(8,128)} fusion(s32[256]{0:T(256)} %bitcast.1001, f32[256,4096]{1,0:T(8,128)} %bitcast.1002, f32[]{:T(128)} %constant.54.clone.1), kind=kCustom, calls=%fused_computation.167 | custom fusion | bytes 8389120 | tf_op jit(solution)/shard_map/scatter | solution.py:214
  284.9 10.6 %reshape.1770 = f32[64,4,2,4096]{3,2,1,0:T(2,128)} reshape(f32[512,4096]{1,0:T(8,128)} %scatter_custom_fusion.2) | data formatting | bytes 16777216 | tf_op jit(solution)/shard_map/reshape | solution.py:222
  295.5 10.5 %all-to-all-start.4 = ((f32[64,4,2,4096]{3,2,1,0:T(2,128)}), f32[64,4,2,4096]{3,2,1,0:T(2,128)}, u32[]{:S(2)}, u32[]{:S(2)}) async-start(f32[64,4,2,4096]{3,2,1,0:T(2,128)} %reshape.1770), calls=%async_computation.4 | async-start | bytes 16777216 | tf_op jit(solution)/shard_map/all_to_all | solution.py:221
  308.6 178.9 %all-to-all-done.4 = f32[64,4,2,4096]{3,2,1,0:T(2,128)} async-done(((f32[64,4,2,4096]{3,2,1,0:T(2,128)}), f32[64,4,2,4096]{3,2,1,0:T(2,128)}, u32[]{:S(2)}, u32[]{:S(2)}) %all-to-all-start.4) | async-done | bytes 8388640 | tf_op jit(solution)/shard_map/all_to_all | solution.py:221
  487.6 4.2 all-to-all-start.3
  491.8 7.4 copy.83
  499.2 5.7 all-to-all-start.5
  504.9 3.3 collective-permute-start
  508.2 1.9 collective-permute-start.1
  510.2 85.5 %collective-permute-done = f32[4,1]{1,0:T(4,128)S(1)} collective-permute-done((f32[4,1]{1,0:T(4,128)S(1)}, f32[4,1]{1,0:T(4,128)S(1)}, u32[]{:S(2)}, u32[]{:S(2)}) %collective-permute-start) | collective-permute-done | bytes 48 | tf_op jit(solution)/shard_map/ppermute | solution.py:23
  596.4 1.2 reduce.99
  599.8 7.6 %copy.84 = f32[64,4,2,4096]{3,2,1,0:T(2,128)} copy(f32[64,4,2,4096]{3,2,0,1:T(2,128)} %all-to-all-done.5) | data formatting | bytes 16777216 | tf_op jit(solution)/shard_map/all_to_all | solution.py:220
  607.4 10.9 %reshape.1771 = f32[512,4096]{1,0:T(8,128)} reshape(f32[64,4,2,4096]{3,2,1,0:T(2,128)} %copy.84) | data formatting | bytes 16777216 | tf_op jit(solution)/shard_map/reshape | solution.py:251
  618.3 9.0 %copy.85 = f32[4096,512]{1,0:T(8,128)} copy(f32[4096,512]{0,1:T(8,128)} %bitcast.915) | data formatting | bytes 16777216 | tf_op jit(solution)/shard_map/dot_general | solution.py:249
  627.3 17.0 %convolution_bitcast_fusion = f32[16,4,4,16,16]{4,0,2,3,1:T(8,128)S(1)} fusion(f32[4,16,4,16,512]{4,3,2,1,0:T(8,128)} %bitcast.914, s32[512]{0:T(512)S(1)} %eq.99), kind=kOutput, calls=%fused_computation.169 | convolution fusion | flops 402661376 | bytes 8652800 | tf_op jit(solution)/shard_map/dot_general | solution.py:249
  644.3 1.9 copy.86
  646.2 2.3 gather_fusion.2
  648.6 2.3 gather_fusion.3
  651.1 2.3 gather_fusion.4
  654.0 2.3 gather_fusion.1
  658.6 5.3 collective-permute-start.2
  664.0 1.9 collective-permute-start.3
  665.9 8.4 %collective-permute-done.3 = f32[4,1]{1,0:T(4,128)S(1)} collective-permute-done((f32[4,1]{1,0:T(4,128)S(1)}, f32[4,1]{1,0:T(4,128)S(1)}, u32[]{:S(2)}, u32[]{:S(2)}) %collective-permute-start.3) | collective-permute-done | bytes 48 | tf_op jit(solution)/shard_map/ppermute | solution.py:24
  676.7 1.9 collective-permute-start.4
  678.6 3.3 collective-permute-start.5
  682.0 7.0 collective-permute-done.5
  691.3 1.9 collective-permute-start.6
  693.3 3.6 collective-permute-start.7
  696.9 6.7 collective-permute-done.7
  706.0 1.9 collective-permute-start.8
  708.0 3.3 collective-permute-start.9
  711.3 7.0 collective-permute-done.9
  720.7 1.9 collective-permute-start.10
  722.7 3.3 collective-permute-start.11
  726.0 7.0 collective-permute-done.11
  (477 shorter events, 69.2 us)
Async XLA Ops:
  7.2 108.6 %all-gather.2.cloned.1.call-start = ((), (), s32[]{:S(2)}) async-start(), calls=%async_computation.6 | async-start | bytes 1052672 | tf_op jit(solution)/shard_map/all_gather | solution.py:196
  10.9 0.6 copy-start.16
  14.2 20.7 %all-to-all-start = ((s32[64,4,2]{1,2,0:T(2,128)}), s32[64,4,2]{1,2,0:T(2,128)S(1)}, u32[]{:S(2)}, u32[]{:S(2)}) async-start(s32[64,4,2]{1,2,0:T(2,128)} %copy.75), calls=%async_computation | async-start | bytes 131072 | tf_op jit(solution)/shard_map/all_to_all | solution.py:184
  35.7 232.2 %all-to-all-start.1 = ((s32[4,1,128]{2,1,0:T(1,128)}), s32[4,1,128]{2,1,0:T(1,128)}, u32[]{:S(2)}, u32[]{:S(2)}) async-start(s32[4,1,128]{2,1,0:T(1,128)} %reshape.1949), calls=%async_computation.1 | async-start | bytes 4096 | tf_op jit(solution)/shard_map/all_to_all | solution.py:183
  146.8 0.6 copy-start.1
  146.9 0.6 copy-start.2
  146.9 0.6 copy-start.3
  146.9 0.6 copy-start.4
  146.9 0.6 copy-start.5
  146.9 0.6 copy-start.7
  146.9 0.6 copy-start.8
  146.9 0.6 copy-start.9
  146.9 0.6 copy-start.10
  147.0 0.6 copy-start.12
  147.0 0.6 copy-start.13
  178.1 0.6 copy-start.1
  178.1 0.6 copy-start.2
  178.1 0.6 copy-start.3
  178.2 0.6 copy-start.4
  178.2 0.6 copy-start.5
  178.2 0.6 copy-start.7
  178.2 0.6 copy-start.8
  178.2 0.6 copy-start.9
  178.2 0.6 copy-start.10
  178.2 0.6 copy-start.12
  178.2 0.6 copy-start.13
  209.5 0.6 copy-start.1
  209.5 0.6 copy-start.2
  209.5 0.6 copy-start.3
  209.5 0.6 copy-start.4
  209.5 0.6 copy-start.5
  209.5 0.6 copy-start.7
  209.5 0.6 copy-start.8
  209.6 0.6 copy-start.9
  209.6 0.6 copy-start.10
  209.6 0.6 copy-start.12
  209.6 0.6 copy-start.13
  240.7 0.6 copy-start.1
  240.8 0.6 copy-start.2
  240.8 0.6 copy-start.3
  240.8 0.6 copy-start.4
  240.8 0.6 copy-start.5
  240.8 0.6 copy-start.7
  240.8 0.6 copy-start.8
  240.8 0.6 copy-start.9
  240.8 0.6 copy-start.10
  240.9 0.6 copy-start.12
  240.9 0.6 copy-start.13
  267.8 27.6 %all-to-all-start.2 = ((f32[64,1,512]{2,1,0:T(1,128)}), f32[64,1,512]{2,1,0:T(1,128)S(1)}, u32[]{:S(2)}, u32[]{:S(2)}) async-start(f32[64,1,512]{2,1,0:T(1,128)} %reshape.1951), calls=%async_computation.2 | async-start | bytes 262144 | tf_op jit(solution)/shard_map/all_to_all | solution.py:234
  295.5 192.1 %all-to-all-start.4 = ((f32[64,4,2,4096]{3,2,1,0:T(2,128)}), f32[64,4,2,4096]{3,2,1,0:T(2,128)}, u32[]{:S(2)}, u32[]{:S(2)}) async-start(f32[64,4,2,4096]{3,2,1,0:T(2,128)} %reshape.1770), calls=%async_computation.4 | async-start | bytes 16777216 | tf_op jit(solution)/shard_map/all_to_all | solution.py:221
  487.6 11.6 %all-to-all-start.3 = ((f32[4,1,8192]{2,1,0:T(1,128)}), f32[4,1,8192]{2,1,0:T(1,128)S(1)}, u32[]{:S(2)}, u32[]{:S(2)}) async-start(f32[4,1,8192]{2,1,0:T(1,128)} %reshape.1953), calls=%async_computation.3 | async-start | bytes 262144 | tf_op jit(solution)/shard_map/all_to_all | solution.py:233
  499.2 100.6 %all-to-all-start.5 = ((f32[64,4,2,4096]{3,2,0,1:T(2,128)}), f32[64,4,2,4096]{3,2,0,1:T(2,128)}, u32[]{:S(2)}, u32[]{:S(2)}) async-start(f32[64,4,2,4096]{3,2,0,1:T(2,128)} %copy.83), calls=%async_computation.5 | async-start | bytes 16777216 | tf_op jit(solution)/shard_map/all_to_all | solution.py:220
  504.9 90.9 %collective-permute-start = (f32[4,1]{1,0:T(4,128)S(1)}, f32[4,1]{1,0:T(4,128)S(1)}, u32[]{:S(2)}, u32[]{:S(2)}) collective-permute-start(f32[4,1]{1,0:T(4,128)S(1)} %broadcast.741), channel_id=1, source_target_pairs={{0,1},{1,2},{2,3},{3,4},{4,5},{5,6},{6,7},{7,8},{8,9},{9,10},{10,1... | collective-permute-start | bytes 56 | tf_op jit(solution)/shard_map/ppermute | solution.py:23
  508.2 87.5 %collective-permute-start.1 = (f32[4,1]{1,0:T(4,128)S(1)}, f32[4,1]{1,0:T(4,128)S(1)}, u32[]{:S(2)}, u32[]{:S(2)}) collective-permute-start(f32[4,1]{1,0:T(4,128)S(1)} %broadcast.741), channel_id=1, source_target_pairs={{1,0},{2,1},{3,2},{4,3},{5,4},{6,5},{7,6},{8,7},{9,8},{10,9},{11,1... | collective-permute-start | bytes 56 | tf_op jit(solution)/shard_map/ppermute | solution.py:24
  658.6 7.3 collective-permute-start.2
  664.0 10.3 %collective-permute-start.3 = (f32[4,1]{1,0:T(4,128)S(1)}, f32[4,1]{1,0:T(4,128)S(1)}, u32[]{:S(2)}, u32[]{:S(2)}) collective-permute-start(f32[4,1]{1,0:T(4,128)S(1)} %get-tuple-element.277), channel_id=1, source_target_pairs={{1,0},{2,1},{3,2},{4,3},{5,4},{6,5},{7,6},{8,7},{9,8},{10,9},{11,1... | collective-permute-start | bytes 56 | tf_op jit(solution)/shard_map/ppermute | solution.py:24
  676.7 5.3 collective-permute-start.4
  678.6 10.3 %collective-permute-start.5 = (f32[4,1]{1,0:T(4,128)S(1)}, f32[4,1]{1,0:T(4,128)S(1)}, u32[]{:S(2)}, u32[]{:S(2)}) collective-permute-start(f32[4,1]{1,0:T(4,128)S(1)} %get-tuple-element.275), channel_id=1, source_target_pairs={{1,0},{2,1},{3,2},{4,3},{5,4},{6,5},{7,6},{8,7},{9,8},{10,9},{11,1... | collective-permute-start | bytes 56 | tf_op jit(solution)/shard_map/ppermute | solution.py:24
  691.3 5.5 collective-permute-start.6
  693.3 10.3 %collective-permute-start.7 = (f32[4,1]{1,0:T(4,128)S(1)}, f32[4,1]{1,0:T(4,128)S(1)}, u32[]{:S(2)}, u32[]{:S(2)}) collective-permute-start(f32[4,1]{1,0:T(4,128)S(1)} %get-tuple-element.273), channel_id=1, source_target_pairs={{1,0},{2,1},{3,2},{4,3},{5,4},{6,5},{7,6},{8,7},{9,8},{10,9},{11,1... | collective-permute-start | bytes 56 | tf_op jit(solution)/shard_map/ppermute | solution.py:24
  706.0 5.3 collective-permute-start.8
  708.0 10.3 %collective-permute-start.9 = (f32[4,1]{1,0:T(4,128)S(1)}, f32[4,1]{1,0:T(4,128)S(1)}, u32[]{:S(2)}, u32[]{:S(2)}) collective-permute-start(f32[4,1]{1,0:T(4,128)S(1)} %get-tuple-element.271), channel_id=1, source_target_pairs={{1,0},{2,1},{3,2},{4,3},{5,4},{6,5},{7,6},{8,7},{9,8},{10,9},{11,1... | collective-permute-start | bytes 56 | tf_op jit(solution)/shard_map/ppermute | solution.py:24
  720.7 5.3 collective-permute-start.10
  722.7 10.3 %collective-permute-start.11 = (f32[4,1]{1,0:T(4,128)S(1)}, f32[4,1]{1,0:T(4,128)S(1)}, u32[]{:S(2)}, u32[]{:S(2)}) collective-permute-start(f32[4,1]{1,0:T(4,128)S(1)} %get-tuple-element.269), channel_id=1, source_target_pairs={{1,0},{2,1},{3,2},{4,3},{5,4},{6,5},{7,6},{8,7},{9,8},{10,9},{11,1... | collective-permute-start | bytes 56 | tf_op jit(solution)/shard_map/ppermute | solution.py:24
  (20 other events, 11.0 us)
Sparse Core Ops, SparseCore 0:
  11.7 103.9 all-gather.1
where the time goes:
time: 751 us; the launch traced here: 741 us
  waiting for transfers between devices  377 us (50%)
  local copies, waits for them, and re-layouts  148 us (20%)
  matrix products  97.9 us (13%)
  starting transfers between devices  78.2 us (10%)
  other arithmetic  23.7 us (3%)
  between operations  15.1 us (2%)
    all_to_all x1, waiting for transfers between devices, per_device(): lax.all_to_all(outgoing.reshape(cell_groups, time_groups, capacity, paylo...  179 us
    ppermute x6, waiting for transfers between devices, padded_2(): before = lax.ppermute(last, axis, up)  85.5 us
    all_gather x1, waiting for transfers between devices, per_device(): whole = lax.all_gather(attitude, ('cells', 'tm'), axis=1, tiled=True)  75.8 us
    dot_general x4, matrix products, cell_work(): gradient = jnp.einsum('tmas,ts->tma', rows, second, precision=highest)  58.7 us
    ppermute x6, waiting for transfers between devices, padded_2(): after = lax.ppermute(leading, axis, down)  36.1 us
    reshape x2, local copies, waits for them, and re-layouts, per_device(): values = whole.reshape(4, -1, KB)[:, global_ids, :].transpose(1, 0, 2)  19.2 us
    ppermute x6, starting transfers between devices, padded_2(): after = lax.ppermute(leading, axis, down)  17.4 us
    dot_general x1, matrix products, per_device(): jnp.dot(member, arrived.reshape(devices * capacity, payload.shape[1]), pr...  17 us
  transfers between devices with their start and end apart: 19, of which 8 were waited for; matrix products, arithmetic and copies ran while one was open for 27% of the time, Pallas kernels for 0%

commit v1 on v0

--- a/solution.py
+++ b/solution.py
@@ -193,7 +193,12 @@
         concat_axis=1,
         tiled=True,
     )
-    whole = lax.all_gather(attitude, ("cells", "tm"), axis=1, tiled=True)
+    whole = jnp.concatenate(
+        lax.all_to_all(
+            jnp.stack([attitude] * lax.axis_size(("cells", "tm"))), ("cells", "tm"), 0, 0
+        ),
+        axis=1,
+    )
     global_ids = owners * blocks_here + slots
     values = whole.reshape(4, -1, KB)[:, global_ids, :].transpose(1, 0, 2)
     transit = lax.broadcasted_iota(jnp.int32, (cells_here, transits), 1)

time: 751 us -> 692 us (0.921)
  waiting for transfers between devices: 377 us -> 320 us
  blocking collectives: 0 us -> 16.3 us
  between operations: 15.1 us -> 1.74 us
    all_gather x1 -> x0, waiting for transfers between devices: 75.8 us -> none  [per_device(): whole = lax.all_gather(attitude, ('cells', 'tm'), axis=1, tiled=True)]
    all_to_all x1, waiting for transfers between devices: 0.01 us -> 19 us  [per_device(): lax.all_to_all(jnp.stack([attitude] * lax.axis_size(('cells', 'tm'))), ('...]
    reshape x2 -> x1, local copies, waits for them, and re-layouts: 19.2 us -> 0.2 us  [per_device(): jnp.concatenate(lax.all_to_all(jnp.stack([attitude] * lax.axis_size(('cel...]
    another operation x1 -> x4, local copies, waits for them, and re-layouts: 0.01 us -> 18.3 us  [the longest x2 16.5 us: per_device(): values = whole.reshape(4, -1, KB)[:, global_ids, :].transpose(1, 0, 2)]
    all_to_all x0 -> x1, blocking collectives: none -> 16.3 us  [per_device(): lax.all_to_all(requests.reshape(cell_groups, time_groups, capacity), 'cel...]
  transfers between devices with their start and end apart: 19 -> 18, of which waited for: 8 -> 8; matrix products, arithmetic and copies ran while one was open for 27% -> 27% of each run, Pallas kernels for 0% -> 0%
where the time goes in v1:
time: 692 us; the launch traced here: 683 us
  waiting for transfers between devices  320 us (46%)
  local copies, waits for them, and re-layouts  143 us (21%)
  matrix products  97.9 us (14%)
  starting transfers between devices  80.1 us (12%)
  other arithmetic  23 us (3%)
  blocking collectives  16.3 us (2%)
    all_to_all x1, waiting for transfers between devices, per_device(): lax.all_to_all(outgoing.reshape(cell_groups, time_groups, capacity, paylo...  179 us
    ppermute x6, waiting for transfers between devices, padded_2(): before = lax.ppermute(last, axis, up)  85.5 us
    dot_general x4, matrix products, cell_work(): gradient = jnp.einsum('tmas,ts->tma', rows, second, precision=highest)  58.7 us
    ppermute x6, waiting for transfers between devices, padded_2(): after = lax.ppermute(leading, axis, down)  36.1 us
    all_to_all x1, waiting for transfers between devices, per_device(): lax.all_to_all(jnp.stack([attitude] * lax.axis_size(('cells', 'tm'))), ('...  19 us
    ppermute x6, starting transfers between devices, padded_2(): after = lax.ppermute(leading, axis, down)  17.4 us
    dot_general x1, matrix products, per_device(): jnp.dot(member, arrived.reshape(devices * capacity, payload.shape[1]), pr...  17 us
    another operation x2, local copies, waits for them, and re-layouts, per_device(): values = whole.reshape(4, -1, KB)[:, global_ids, :].transpose(1, 0, 2)  16.5 us
  transfers between devices with their start and end apart: 18, of which 8 were waited for; matrix products, arithmetic and copies ran while one was open for 27% of the time, Pallas kernels for 0%

profile of v1, /device:TPU:127, one launch (start us, length us, event | category | flops | bytes accessed | tf_op | source)
XLA Modules:
  0.0 683.1 jit_solution(2052122918424182578)
XLA Ops:
  1.2 1.4 fusion.207
  4.2 1.4 scatter_custom_fusion
  6.4 16.3 %all_to_all.35 = s32[64,4,2]{1,2,0:T(2,128)S(1)} all-to-all(s32[64,4,2]{1,2,0:T(2,128)S(1)} %copy.77), channel_id=1, replica_groups=mesh['cells'=64,'tm'=4] {'cells'}, dimensions={0} | all-to-all | bytes 4096 | tf_op jit(solution)/shard_map/all_to_all | solution.py:184
  22.7 1.8 stack.76
  24.5 11.3 %all-to-all-start = ((f32[256,4,256]{2,1,0:T(4,128)}), f32[256,4,256]{2,1,0:T(4,128)S(1)}, u32[]{:S(2)}, u32[]{:S(2)}) async-start(f32[256,4,256]{2,1,0:T(4,128)} %stack.76), calls=%async_computation | async-start | bytes 2097152 | tf_op jit(solution)/shard_map/all_to_all | solution.py:197
  36.7 2.1 reshape.1757
  42.0 19.0 %all-to-all-done = f32[256,4,256]{2,1,0:T(4,128)S(1)} async-done(((f32[256,4,256]{2,1,0:T(4,128)}), f32[256,4,256]{2,1,0:T(4,128)S(1)}, u32[]{:S(2)}, u32[]{:S(2)}) %all-to-all-start) | async-done | bytes 1048608 | tf_op jit(solution)/shard_map/all_to_all | solution.py:197
  61.1 6.1 all-to-all-start.2
  67.3 4.7 reshape_reshape.3
  72.0 11.8 %copy.69 = f32[4,4096,16]{2,0,1:T(4,128)} copy(f32[4,4096,16]{2,1,0:T(8,128)} %reshape_reshape.3) | data formatting | bytes 2097152 | tf_op jit(solution)/shard_map/reshape;reshape | solution.py:203
  83.8 4.4 gather_fusion
  88.4 125.9 %while.14 = (s32[]{:T(128)}, f32[4,5,128]{2,1,0:T(8,128)}, f32[4,64,4096]{2,1,0:T(8,128)}, f32[4,64,64]{2,1,0:T(8,128)}, f32[4,5,64,128]{3,0,2,1:T(4,128)}, /*in...) while((s32[]{:T(128)}, f32[4,5,128]{2,1,0:T(8,128)}, ...), condition=%wide.region_21.22_spmd, body=%wide.region_0.21_spmd.sunk | while | flops 419069696 | bytes 14432589 | solution.py:215
  92.3 2.0 fusion.265
  94.4 1.2 constant_dynamic-slice_fusion.10
  96.5 14.7 %fusion.269 = f32[64,1,4,16]{3,1,2,0:T(1,128)S(1)} fusion(f32[64,128,1,1]{1,2,3,0:T(1,128)S(1)} %bitcast.975, f32[64,16,128]{2,1,0:T(8,128)S(1)} %add_multiply_fusion.2, f32[64,4,128]{2,1,0:T(4,128)S(1)} %bitcast.954), kind=kOutput, calls=%fused_computation.8.clone.1 | convolution fusion | flops 6815744 | bytes 704512 | tf_op jit(solution)/shard_map/while/body/eval_jaxpr/tmas,ts->tma/dot_general | solution.py:148
  112.3 3.4 fusion.268
  123.6 2.0 fusion.265
  125.7 1.2 constant_dynamic-slice_fusion.10
  127.8 14.7 %fusion.269 = f32[64,1,4,16]{3,1,2,0:T(1,128)S(1)} fusion(f32[64,128,1,1]{1,2,3,0:T(1,128)S(1)} %bitcast.975, f32[64,16,128]{2,1,0:T(8,128)S(1)} %add_multiply_fusion.2, f32[64,4,128]{2,1,0:T(4,128)S(1)} %bitcast.954), kind=kOutput, calls=%fused_computation.8.clone.1 | convolution fusion | flops 6815744 | bytes 704512 | tf_op jit(solution)/shard_map/while/body/eval_jaxpr/tmas,ts->tma/dot_general | solution.py:148
  143.6 3.4 fusion.268
  155.0 2.0 fusion.265
  159.1 14.7 %fusion.269 = f32[64,1,4,16]{3,1,2,0:T(1,128)S(1)} fusion(f32[64,128,1,1]{1,2,3,0:T(1,128)S(1)} %bitcast.975, f32[64,16,128]{2,1,0:T(8,128)S(1)} %add_multiply_fusion.2, f32[64,4,128]{2,1,0:T(4,128)S(1)} %bitcast.954), kind=kOutput, calls=%fused_computation.8.clone.1 | convolution fusion | flops 6815744 | bytes 704512 | tf_op jit(solution)/shard_map/while/body/eval_jaxpr/tmas,ts->tma/dot_general | solution.py:148
  174.9 3.4 fusion.268
  186.2 2.0 fusion.265
  188.3 1.2 constant_dynamic-slice_fusion.10
  190.4 14.7 %fusion.269 = f32[64,1,4,16]{3,1,2,0:T(1,128)S(1)} fusion(f32[64,128,1,1]{1,2,3,0:T(1,128)S(1)} %bitcast.975, f32[64,16,128]{2,1,0:T(8,128)S(1)} %add_multiply_fusion.2, f32[64,4,128]{2,1,0:T(4,128)S(1)} %bitcast.954), kind=kOutput, calls=%fused_computation.8.clone.1 | convolution fusion | flops 6815744 | bytes 704512 | tf_op jit(solution)/shard_map/while/body/eval_jaxpr/tmas,ts->tma/dot_general | solution.py:148
  206.2 3.4 fusion.268
  214.3 1.6 scatter_custom_fusion.1
  216.8 8.4 %all-to-all-start.3 = ((f32[64,1,512]{2,1,0:T(1,128)}), f32[64,1,512]{2,1,0:T(1,128)S(1)}, u32[]{:S(2)}, u32[]{:S(2)}) async-start(f32[64,1,512]{2,1,0:T(1,128)} %reshape.1953), calls=%async_computation.3 | async-start | bytes 262144 | tf_op jit(solution)/shard_map/all_to_all | solution.py:239
  225.2 8.2 %scatter_custom_fusion.2 = f32[512,4096]{1,0:T(8,128)} fusion(s32[256]{0:T(256)} %bitcast.1003, f32[256,4096]{1,0:T(8,128)} %bitcast.1004, f32[]{:T(128)} %constant.54.clone.1), kind=kCustom, calls=%fused_computation.167 | custom fusion | bytes 8389120 | tf_op jit(solution)/shard_map/scatter | solution.py:219
  233.5 10.6 %reshape.1772 = f32[64,4,2,4096]{3,2,1,0:T(2,128)} reshape(f32[512,4096]{1,0:T(8,128)} %scatter_custom_fusion.2) | data formatting | bytes 16777216 | tf_op jit(solution)/shard_map/reshape | solution.py:227
  244.0 10.5 %all-to-all-start.5 = ((f32[64,4,2,4096]{3,2,1,0:T(2,128)}), f32[64,4,2,4096]{3,2,1,0:T(2,128)}, u32[]{:S(2)}, u32[]{:S(2)}) async-start(f32[64,4,2,4096]{3,2,1,0:T(2,128)} %reshape.1772), calls=%async_computation.5 | async-start | bytes 16777216 | tf_op jit(solution)/shard_map/all_to_all | solution.py:226
  257.2 178.9 %all-to-all-done.5 = f32[64,4,2,4096]{3,2,1,0:T(2,128)} async-done(((f32[64,4,2,4096]{3,2,1,0:T(2,128)}), f32[64,4,2,4096]{3,2,1,0:T(2,128)}, u32[]{:S(2)}, u32[]{:S(2)}) %all-to-all-start.5) | async-done | bytes 8388640 | tf_op jit(solution)/shard_map/all_to_all | solution.py:226
  436.1 4.2 all-to-all-start.4
  440.4 7.4 %copy.85 = f32[64,4,2,4096]{3,2,0,1:T(2,128)} copy(f32[64,4,2,4096]{3,2,1,0:T(2,128)} %all-to-all-done.5) | data formatting | bytes 16777216 | tf_op jit(solution)/shard_map/all_to_all | solution.py:226
  447.8 5.7 all-to-all-start.6
  453.4 3.3 collective-permute-start
  456.8 1.9 collective-permute-start.1
  458.8 85.5 %collective-permute-done = f32[4,1]{1,0:T(4,128)S(1)} collective-permute-done((f32[4,1]{1,0:T(4,128)S(1)}, f32[4,1]{1,0:T(4,128)S(1)}, u32[]{:S(2)}, u32[]{:S(2)}) %collective-permute-start) | collective-permute-done | bytes 48 | tf_op jit(solution)/shard_map/ppermute | solution.py:23
  545.0 1.2 reduce.99
  548.4 7.6 %copy.86 = f32[64,4,2,4096]{3,2,1,0:T(2,128)} copy(f32[64,4,2,4096]{3,2,0,1:T(2,128)} %all-to-all-done.6) | data formatting | bytes 16777216 | tf_op jit(solution)/shard_map/all_to_all | solution.py:225
  556.0 10.9 %reshape.1773 = f32[512,4096]{1,0:T(8,128)} reshape(f32[64,4,2,4096]{3,2,1,0:T(2,128)} %copy.86) | data formatting | bytes 16777216 | tf_op jit(solution)/shard_map/reshape | solution.py:256
  566.9 9.0 %copy.87 = f32[4096,512]{1,0:T(8,128)} copy(f32[4096,512]{0,1:T(8,128)} %bitcast.916) | data formatting | bytes 16777216 | tf_op jit(solution)/shard_map/dot_general | solution.py:254
  575.9 17.0 %convolution_bitcast_fusion = f32[16,4,4,16,16]{4,0,2,3,1:T(8,128)S(1)} fusion(f32[4,16,4,16,512]{4,3,2,1,0:T(8,128)} %bitcast.915, s32[512]{0:T(512)S(1)} %eq.99), kind=kOutput, calls=%fused_computation.169 | convolution fusion | flops 402661376 | bytes 8652800 | tf_op jit(solution)/shard_map/dot_general | solution.py:254
  592.9 1.9 copy.88
  594.8 2.3 gather_fusion.2
  597.2 2.3 gather_fusion.3
  599.7 2.3 gather_fusion.4
  602.6 2.3 gather_fusion.1
  607.2 5.3 collective-permute-start.2
  612.6 1.9 collective-permute-start.3
  614.5 8.4 %collective-permute-done.3 = f32[4,1]{1,0:T(4,128)S(1)} collective-permute-done((f32[4,1]{1,0:T(4,128)S(1)}, f32[4,1]{1,0:T(4,128)S(1)}, u32[]{:S(2)}, u32[]{:S(2)}) %collective-permute-start.3) | collective-permute-done | bytes 48 | tf_op jit(solution)/shard_map/ppermute | solution.py:24
  625.3 1.9 collective-permute-start.4
  627.2 3.3 collective-permute-start.5
  630.6 7.0 %collective-permute-done.5 = f32[4,1]{1,0:T(4,128)S(1)} collective-permute-done((f32[4,1]{1,0:T(4,128)S(1)}, f32[4,1]{1,0:T(4,128)S(1)}, u32[]{:S(2)}, u32[]{:S(2)}) %collective-permute-start.5) | collective-permute-done | bytes 48 | tf_op jit(solution)/shard_map/ppermute | solution.py:24
  639.9 1.9 collective-permute-start.6
  641.9 3.6 collective-permute-start.7
  645.5 6.7 collective-permute-done.7
  654.6 1.9 collective-permute-start.8
  656.5 3.3 collective-permute-start.9
  659.9 7.0 %collective-permute-done.9 = f32[4,1]{1,0:T(4,128)S(1)} collective-permute-done((f32[4,1]{1,0:T(4,128)S(1)}, f32[4,1]{1,0:T(4,128)S(1)}, u32[]{:S(2)}, u32[]{:S(2)}) %collective-permute-start.9) | collective-permute-done | bytes 48 | tf_op jit(solution)/shard_map/ppermute | solution.py:24
  669.3 1.9 collective-permute-start.10
  671.2 3.3 collective-permute-start.11
  674.6 7.0 %collective-permute-done.11 = f32[4,1]{1,0:T(4,128)S(1)} collective-permute-done((f32[4,1]{1,0:T(4,128)S(1)}, f32[4,1]{1,0:T(4,128)S(1)}, u32[]{:S(2)}, u32[]{:S(2)}) %collective-permute-start.11) | collective-permute-done | bytes 48 | tf_op jit(solution)/shard_map/ppermute | solution.py:24
  (487 shorter events, 67.4 us)
Async XLA Ops:
  0.6 38.2 %copy-start = (f32[4,64,512]{2,1,0:T(8,128)S(1)}, f32[4,64,512]{2,1,0:T(8,128)}, u32[]{:S(2)}) copy-start(f32[4,64,512]{2,1,0:T(8,128)} %param.13) | copy-start | bytes 1572868
  0.6 39.1 %copy-start.1 = (f32[64,512]{1,0:T(8,128)S(1)}, f32[64,512]{1,0:T(8,128)}, u32[]{:S(2)}) copy-start(f32[64,512]{1,0:T(8,128)} %param.14) | copy-start | bytes 393220
  0.7 39.2 %copy-start.2 = (s32[64,512]{1,0:T(8,128)S(1)}, s32[64,512]{1,0:T(8,128)}, u32[]{:S(2)}) copy-start(s32[64,512]{1,0:T(8,128)} %param.16) | copy-start | bytes 393220
  0.7 39.2 %copy-start.3 = (f32[64,512]{1,0:T(8,128)S(1)}, f32[64,512]{1,0:T(8,128)}, u32[]{:S(2)}) copy-start(f32[64,512]{1,0:T(8,128)} %param.15) | copy-start | bytes 393220
  0.7 39.9 %copy-start.21 = (s32[4]{0:T(128)S(1)}, s32[4]{0:T(128)}, u32[]{:S(2)}) copy-start(s32[4]{0:T(128)} %param.17) | copy-start | bytes 52
  3.7 0.6 copy-start.20
  24.5 36.6 %all-to-all-start = ((f32[256,4,256]{2,1,0:T(4,128)}), f32[256,4,256]{2,1,0:T(4,128)S(1)}, u32[]{:S(2)}, u32[]{:S(2)}) async-start(f32[256,4,256]{2,1,0:T(4,128)} %stack.76), calls=%async_computation | async-start | bytes 2097152 | tf_op jit(solution)/shard_map/all_to_all | solution.py:197
  61.1 155.7 %all-to-all-start.2 = ((s32[4,1,128]{2,1,0:T(1,128)}), s32[4,1,128]{2,1,0:T(1,128)}, u32[]{:S(2)}, u32[]{:S(2)}) async-start(s32[4,1,128]{2,1,0:T(1,128)} %reshape.1951), calls=%async_computation.2 | async-start | bytes 4096 | tf_op jit(solution)/shard_map/all_to_all | solution.py:183
  95.8 0.6 copy-start.5
  95.8 0.6 copy-start.6
  95.8 0.6 copy-start.7
  95.8 0.6 copy-start.8
  95.8 0.6 copy-start.11
  95.9 0.6 copy-start.12
  95.9 0.6 copy-start.13
  95.9 0.6 copy-start.14
  95.9 0.6 copy-start.16
  127.1 0.6 copy-start.5
  127.1 0.6 copy-start.6
  127.1 0.6 copy-start.7
  127.1 0.6 copy-start.8
  127.1 0.6 copy-start.9
  127.1 0.6 copy-start.11
  127.1 0.6 copy-start.12
  127.2 0.6 copy-start.13
  127.2 0.6 copy-start.14
  127.2 0.6 copy-start.16
  127.2 0.6 copy-start.17
  158.4 0.6 copy-start.5
  158.4 0.6 copy-start.6
  158.4 0.6 copy-start.7
  158.4 0.6 copy-start.8
  158.5 0.6 copy-start.9
  158.5 0.6 copy-start.11
  158.5 0.6 copy-start.12
  158.5 0.6 copy-start.13
  158.5 0.6 copy-start.14
  158.5 0.6 copy-start.16
  158.5 0.6 copy-start.17
  189.7 0.6 copy-start.5
  189.7 0.6 copy-start.6
  189.7 0.6 copy-start.7
  189.7 0.6 copy-start.8
  189.8 0.6 copy-start.11
  189.8 0.6 copy-start.12
  189.8 0.6 copy-start.13
  189.8 0.6 copy-start.14
  189.8 0.6 copy-start.16
  216.8 27.3 %all-to-all-start.3 = ((f32[64,1,512]{2,1,0:T(1,128)}), f32[64,1,512]{2,1,0:T(1,128)S(1)}, u32[]{:S(2)}, u32[]{:S(2)}) async-start(f32[64,1,512]{2,1,0:T(1,128)} %reshape.1953), calls=%async_computation.3 | async-start | bytes 262144 | tf_op jit(solution)/shard_map/all_to_all | solution.py:239
  244.0 192.1 %all-to-all-start.5 = ((f32[64,4,2,4096]{3,2,1,0:T(2,128)}), f32[64,4,2,4096]{3,2,1,0:T(2,128)}, u32[]{:S(2)}, u32[]{:S(2)}) async-start(f32[64,4,2,4096]{3,2,1,0:T(2,128)} %reshape.1772), calls=%async_computation.5 | async-start | bytes 16777216 | tf_op jit(solution)/shard_map/all_to_all | solution.py:226
  436.1 11.6 %all-to-all-start.4 = ((f32[4,1,8192]{2,1,0:T(1,128)}), f32[4,1,8192]{2,1,0:T(1,128)S(1)}, u32[]{:S(2)}, u32[]{:S(2)}) async-start(f32[4,1,8192]{2,1,0:T(1,128)} %reshape.1955), calls=%async_computation.4 | async-start | bytes 262144 | tf_op jit(solution)/shard_map/all_to_all | solution.py:238
  447.8 100.6 %all-to-all-start.6 = ((f32[64,4,2,4096]{3,2,0,1:T(2,128)}), f32[64,4,2,4096]{3,2,0,1:T(2,128)}, u32[]{:S(2)}, u32[]{:S(2)}) async-start(f32[64,4,2,4096]{3,2,0,1:T(2,128)} %copy.85), calls=%async_computation.6 | async-start | bytes 16777216 | tf_op jit(solution)/shard_map/all_to_all | solution.py:225
  453.4 90.9 %collective-permute-start = (f32[4,1]{1,0:T(4,128)S(1)}, f32[4,1]{1,0:T(4,128)S(1)}, u32[]{:S(2)}, u32[]{:S(2)}) collective-permute-start(f32[4,1]{1,0:T(4,128)S(1)} %broadcast.743), channel_id=1, source_target_pairs={{0,1},{1,2},{2,3},{3,4},{4,5},{5,6},{6,7},{7,8},{8,9},{9,10},{10,1... | collective-permute-start | bytes 56 | tf_op jit(solution)/shard_map/ppermute | solution.py:23
  456.8 87.5 %collective-permute-start.1 = (f32[4,1]{1,0:T(4,128)S(1)}, f32[4,1]{1,0:T(4,128)S(1)}, u32[]{:S(2)}, u32[]{:S(2)}) collective-permute-start(f32[4,1]{1,0:T(4,128)S(1)} %broadcast.743), channel_id=1, source_target_pairs={{1,0},{2,1},{3,2},{4,3},{5,4},{6,5},{7,6},{8,7},{9,8},{10,9},{11,1... | collective-permute-start | bytes 56 | tf_op jit(solution)/shard_map/ppermute | solution.py:24
  607.2 7.3 %collective-permute-start.2 = (f32[4,1]{1,0:T(4,128)S(1)}, f32[4,1]{1,0:T(4,128)S(1)}, u32[]{:S(2)}, u32[]{:S(2)}) collective-permute-start(f32[4,1]{1,0:T(4,128)S(1)} %get-tuple-element.276), channel_id=1, source_target_pairs={{0,1},{1,2},{2,3},{3,4},{4,5},{5,6},{6,7},{7,8},{8,9},{9,10},{10,1... | collective-permute-start | bytes 56 | tf_op jit(solution)/shard_map/ppermute | solution.py:23
  612.6 10.3 %collective-permute-start.3 = (f32[4,1]{1,0:T(4,128)S(1)}, f32[4,1]{1,0:T(4,128)S(1)}, u32[]{:S(2)}, u32[]{:S(2)}) collective-permute-start(f32[4,1]{1,0:T(4,128)S(1)} %get-tuple-element.277), channel_id=1, source_target_pairs={{1,0},{2,1},{3,2},{4,3},{5,4},{6,5},{7,6},{8,7},{9,8},{10,9},{11,1... | collective-permute-start | bytes 56 | tf_op jit(solution)/shard_map/ppermute | solution.py:24
  625.3 5.3 collective-permute-start.4
  627.2 10.3 %collective-permute-start.5 = (f32[4,1]{1,0:T(4,128)S(1)}, f32[4,1]{1,0:T(4,128)S(1)}, u32[]{:S(2)}, u32[]{:S(2)}) collective-permute-start(f32[4,1]{1,0:T(4,128)S(1)} %get-tuple-element.275), channel_id=1, source_target_pairs={{1,0},{2,1},{3,2},{4,3},{5,4},{6,5},{7,6},{8,7},{9,8},{10,9},{11,1... | collective-permute-start | bytes 56 | tf_op jit(solution)/shard_map/ppermute | solution.py:24
  639.9 5.5 collective-permute-start.6
  641.9 10.3 %collective-permute-start.7 = (f32[4,1]{1,0:T(4,128)S(1)}, f32[4,1]{1,0:T(4,128)S(1)}, u32[]{:S(2)}, u32[]{:S(2)}) collective-permute-start(f32[4,1]{1,0:T(4,128)S(1)} %get-tuple-element.273), channel_id=1, source_target_pairs={{1,0},{2,1},{3,2},{4,3},{5,4},{6,5},{7,6},{8,7},{9,8},{10,9},{11,1... | collective-permute-start | bytes 56 | tf_op jit(solution)/shard_map/ppermute | solution.py:24
  654.6 5.3 collective-permute-start.8
  656.5 10.3 %collective-permute-start.9 = (f32[4,1]{1,0:T(4,128)S(1)}, f32[4,1]{1,0:T(4,128)S(1)}, u32[]{:S(2)}, u32[]{:S(2)}) collective-permute-start(f32[4,1]{1,0:T(4,128)S(1)} %get-tuple-element.271), channel_id=1, source_target_pairs={{1,0},{2,1},{3,2},{4,3},{5,4},{6,5},{7,6},{8,7},{9,8},{10,9},{11,1... | collective-permute-start | bytes 56 | tf_op jit(solution)/shard_map/ppermute | solution.py:24
  669.3 5.3 collective-permute-start.10
  671.2 10.3 %collective-permute-start.11 = (f32[4,1]{1,0:T(4,128)S(1)}, f32[4,1]{1,0:T(4,128)S(1)}, u32[]{:S(2)}, u32[]{:S(2)}) collective-permute-start(f32[4,1]{1,0:T(4,128)S(1)} %get-tuple-element.269), channel_id=1, source_target_pairs={{1,0},{2,1},{3,2},{4,3},{5,4},{6,5},{7,6},{8,7},{9,8},{10,9},{11,1... | collective-permute-start | bytes 56 | tf_op jit(solution)/shard_map/ppermute | solution.py:24
  (24 other events, 13.3 us)
